TPU v7x, 128 devices: a whole 4x4x4 slice. The times are simulated.
128 devices in a mesh: left: 8 (over z, core), right: 16 (over y, x).
Axes of the slice: x: 4, y: 4, z: 4, core: 2. Of those that a mesh axis runs over, the one named last changes fastest.
Arguments:
- wavefunction: bfloat16 [10240, 10240], P('left', 'right'), may hold values from -6 to 6
- left_env: bfloat16 [8, 10240, 640], P(None, 'left'), may hold values from -0.25 to 0.25
- right_env: bfloat16 [8, 640, 10240], P(None, None, 'right'), may hold values from -0.25 to 0.25
- left_sizes: int32 [16], replicated, may hold values from 512 to 640, as said below
- right_sizes: int32 [16], replicated, may hold values from 512 to 640, as said below
- allowed: int32 [31], replicated, may hold values 0 or 1
- channel_shift: int32 [8], replicated, may hold values from -1 to 1, as said below
Outputs:
- evolved: bfloat16 [10240, 10240], P('left', 'right')
Inputs may be any that keep to these rules, and one draw needn't show every extreme that they name: `left_sizes`: multiples of 128; in every draw some left sector has exactly 640. `right_sizes`: multiples of 128; in every draw some right sector has exactly 640. `channel_shift`: each of -1, 0 and 1 occurs.
All inputs are finite; a program needn't handle non-finite values.
Results may differ from a plain program's by a relative error of at most 0.0054.
Values may be sent and summed in bfloat16 or wider, within the bound.
A program may use at most 192 MiB of HBM per device.

v0:
```python
import jax
import jax.numpy as jnp
from jax import lax
from jax.experimental import pallas as pl
from jax.experimental.pallas import tpu as pltpu
from jax.sharding import PartitionSpec as P

MAXS = 640
STEPS = 2
WIDTH = 128
PARTS = MAXS // WIDTH
SPLIT = 384
UNROLL = 8

time_step = 0.5

MESH = pl.DeviceIdType.MESH


def kernel(
    left_sizes_in,
    right_sizes_in,
    allowed_in,
    channel_shift_in,
    wave,
    left_env,
    right_env,
    out,
    lbuf,
    rbuf,
    acc,
    half,
    early,
    stage,
    x00,
    x01,
    x10,
    x11,
    left_sizes,
    right_sizes,
    allowed,
    channel_shift,
    small_sem,
    wave_sem,
    left_sem,
    right_sem,
    send_sem,
    recv_sem,
):
    xs = ((x00, x01), (x10, x11))
    channels = lbuf.shape[1]
    rows, cols = lax.axis_size("left"), lax.axis_size("right")
    me, col = lax.axis_index("left"), lax.axis_index("right")
    up, down = lax.rem(me + rows - 1, rows), lax.rem(me + 1, rows)
    before, after = lax.rem(col + cols - 1, cols), lax.rem(col + 1, cols)

    def columns(c):
        return pl.ds(c * WIDTH if isinstance(c, int) else pl.multiple_of(c * WIDTH, WIDTH), WIDTH)

    def fetch_wave(b, c):
        return pltpu.make_async_copy(
            wave.at[pl.ds(b * MAXS, MAXS), columns(c)], xs[0][b].at[c, 1], wave_sem.at[b, c]
        )

    def fetch_left(b):
        return pltpu.make_async_copy(left_env.at[:, pl.ds(b * MAXS, MAXS), :], lbuf.at[b], left_sem.at[b])

    def fetch_right(c):
        return pltpu.make_async_copy(right_env.at[:, columns(c), :], rbuf.at[c], right_sem.at[c])

    small = [
        pltpu.make_async_copy(source, target, small_sem.at[i])
        for i, (source, target) in enumerate(
            (
                (left_sizes_in, left_sizes),
                (right_sizes_in, right_sizes),
                (allowed_in, allowed),
                (channel_shift_in, channel_shift),
            )
        )
    ]
    for copy in small:
        copy.start()
    for b in (1, 0):
        for c in range(PARTS):
            fetch_wave(b, c).start()
    fetch_left(0).start()
    for c in range(PARTS):
        fetch_right(c).start()
    fetch_left(1).start()

    barrier = pltpu.get_barrier_semaphore()
    for peer in ((me, before), (up, after), (down, before), (me, after)):
        pl.semaphore_signal(barrier, inc=1, device_id=peer, device_id_type=MESH)
    pl.semaphore_wait(barrier, 4)

    def pieces(t, b, c):
        if t == STEPS - 1 and b == 1 and isinstance(c, int) and c == PARTS - 1:
            return ((c, 0, SPLIT), (PARTS, SPLIT, MAXS - SPLIT))
        return ((c, 0, MAXS),)

    def copies(t, b, c, piece):
        index, first, count = piece
        targets = ((2, (me if b == 0 else down, before)), (0, (up if b == 0 else me, after)))
        return [
            pltpu.make_async_remote_copy(
                src_ref=xs[t][b].at[c, 1, pl.ds(first, count)],
                dst_ref=xs[t][1 - b].at[c, slot, pl.ds(first, count)],
                send_sem=send_sem.at[t, b, index, side],
                recv_sem=recv_sem.at[t, 1 - b, index, side],
                device_id=target,
                device_id_type=MESH,
            )
            for side, (slot, target) in enumerate(targets)
        ]

    def push(t, b, c):
        for piece in pieces(t, b, c):
            for copy in copies(t, b, c, piece):
                copy.start()

    def arrive(t, b, c, piece):
        for copy in copies(t, 1 - b, c, piece):
            copy.wait_recv()

    def put(t, b, c, piece):
        span = pl.ds(piece[1], piece[2])
        for slot in range(3):
            stage[slot, span, :] = xs[t][b][c, slot, span, :]
        no_after, no_before = col == cols - 1, col == 0
        if b == 0:
            no_after = no_after | (me == 0)
        else:
            no_before = no_before | (me == rows - 1)
        for slot, missing in ((2, no_after), (0, no_before)):

            @pl.when(missing)
            def _():
                stage[slot, span, :] = jnp.zeros((piece[2], WIDTH), jnp.bfloat16)

    def keep(b, c):
        sector = 2 * me + b
        row = lax.broadcasted_iota(jnp.int32, (MAXS, WIDTH), 0)
        column = lax.broadcasted_iota(jnp.int32, (MAXS, WIDTH), 1) + c * WIDTH
        row_limit = jnp.where(allowed[sector + col] == 1, left_sizes[sector], 0)
        return (row < row_limit) & (column < right_sizes[col])

    def each_channel(step):
        lax.fori_loop(0, channels, step, 0, unroll=UNROLL)

    def first_product(b):
        def channel(w, carry):
            product = jnp.dot(lbuf[b, w], stage[channel_shift[w] + 1], preferred_element_type=jnp.float32)
            half[:, columns(w)] = product.astype(jnp.bfloat16)
            return carry

        each_channel(channel)

    def second_product(c):
        return jnp.dot(
            half[...], rbuf[c].reshape(channels * WIDTH, MAXS), preferred_element_type=jnp.float32
        )

    def finish(t, b, total):
        for c in range(PARTS):
            value = xs[t][b][c, 1].astype(jnp.float32) - time_step * total[:, c * WIDTH : (c + 1) * WIDTH]
            value = jnp.where(keep(b, c), value, 0.0).astype(jnp.bfloat16)
            if t == 0:
                xs[1][b][c, 1] = value
            else:
                out[b * MAXS : (b + 1) * MAXS, c * WIDTH : (c + 1) * WIDTH] = value

    for copy in small:
        copy.wait()
    for b in (1, 0):

        def begin(c, carry):
            fetch_wave(b, c).wait()
            value = xs[0][b][c, 1].astype(jnp.float32)
            xs[0][b][c, 1] = jnp.where(keep(b, c), value, 0.0).astype(jnp.bfloat16)
            if b == 1:
                push(0, 1, c)
            return carry

        lax.fori_loop(0, PARTS, begin, 0)

    for t, b, follow in ((0, 0, (0, 0)), (0, 1, (1, 0)), (1, 1, (1, 1)), (1, 0, None)):
        if t == 0:
            fetch_left(b).wait()

        def take(c, piece):
            arrive(t, b, c, piece)
            if follow is not None and piece[0] is c:
                push(*follow, c)
            if t == 0 and b == 0:
                fetch_right(c).wait()
            put(t, b, c, piece)

        acc[...] = jnp.zeros(acc.shape, jnp.float32)

        def absorb(c, carry):
            take(c, (c, 0, MAXS))
            first_product(b)
            acc[...] += second_product(c)
            return carry

        lax.fori_loop(0, PARTS - 1, absorb, 0)
        last = PARTS - 1
        if (t, b) != (STEPS - 1, 0):
            take(last, (last, 0, MAXS))
            first_product(b)
        else:
            top, rest = pieces(t, 1 - b, last)
            take(last, top)

            def early_channel(w, carry):
                early[:, columns(w)] = jnp.dot(
                    lbuf[b, w, :, :SPLIT],
                    stage[channel_shift[w] + 1, :SPLIT],
                    preferred_element_type=jnp.float32,
                )
                return carry

            each_channel(early_channel)
            take(last, rest)

            def late_channel(w, carry):
                product = jnp.dot(
                    lbuf[b, w, :, SPLIT:],
                    stage[channel_shift[w] + 1, SPLIT:],
                    preferred_element_type=jnp.float32,
                )
                half[:, columns(w)] = (early[:, columns(w)] + product).astype(jnp.bfloat16)
                return carry

            each_channel(late_channel)
        finish(t, b, acc[...] + second_product(last))

    for t in range(STEPS):
        for b in range(2):
            for c in range(PARTS):
                for piece in pieces(t, b, c):
                    for copy in copies(t, b, c, piece):
                        copy.wait_send()


def body(wavefunction, left_env, right_env, left_sizes, right_sizes, allowed, channel_shift):
    channels = left_env.shape[0]
    arguments = (left_sizes, right_sizes, allowed, channel_shift, wavefunction, left_env, right_env)
    return pl.pallas_call(
        kernel,
        out_shape=jax.ShapeDtypeStruct(wavefunction.shape, jnp.bfloat16),
        in_specs=[pl.BlockSpec(memory_space=pl.ANY)] * len(arguments),
        out_specs=pl.BlockSpec(memory_space=pltpu.VMEM),
        scratch_shapes=[
            pltpu.VMEM((2, channels, MAXS, MAXS), jnp.bfloat16),
            pltpu.VMEM((PARTS, channels, WIDTH, MAXS), jnp.bfloat16),
            pltpu.VMEM((MAXS, MAXS), jnp.float32),
            pltpu.VMEM((MAXS, channels * WIDTH), jnp.bfloat16),
            pltpu.VMEM((MAXS, channels * WIDTH), jnp.float32),
            pltpu.VMEM((3, MAXS, WIDTH), jnp.bfloat16),
            *[pltpu.VMEM((PARTS, 3, MAXS, WIDTH), jnp.bfloat16)] * 4,
            *[pltpu.SMEM(v.shape, v.dtype) for v in arguments[:4]],
            pltpu.SemaphoreType.DMA((4,)),
            pltpu.SemaphoreType.DMA((2, PARTS)),
            pltpu.SemaphoreType.DMA((2,)),
            pltpu.SemaphoreType.DMA((PARTS,)),
            pltpu.SemaphoreType.DMA((STEPS, 2, PARTS + 1, 2)),
            pltpu.SemaphoreType.DMA((STEPS, 2, PARTS + 1, 2)),
        ],
        compiler_params=pltpu.CompilerParams(
            collective_id=0, has_side_effects=True, vmem_limit_bytes=52 * 2**20
        ),
        name="taylor",
    )(*[pltpu.with_memory_space_constraint(v, pltpu.HBM) for v in arguments])


def solution(mesh):
    return jax.shard_map(
        body,
        mesh=mesh,
        in_specs=(P("left", "right"), P(None, "left", None), P(None, None, "right"), P(), P(), P(), P()),
        out_specs=P("left", "right"),
        check_vma=False,
    )
```

profile of v0, /device:TPU:0, one launch (start us, length us, event | category | flops | bytes accessed | tf_op | source)
XLA Modules:
  0.0 85.5 jit_solution(327996722516390415)
XLA Ops:
  0.0 84.4 %taylor.1 = bf16[1280,640]{1,0:T(8,128)(2,1)S(1)} custom-call(s32[16]{0:T(128)} %left_sizes_in.1, s32[16]{0:T(128)} %right_sizes_in.1, s32[31]{0:T(128)} %allowed_in.1, s32[8]{0:T(128)} %channel_shift_in.1, bf16[1280,640]{1,0:T(8,128)(2,1)} %wave.1, bf16[8,1280,640]{2,1,0:T(8,128)(2,1)} %left_env.1, bf16[8,640,640]{2,1,0:T(8,128)(2,1)} %right_env.1), custom_call_target="tpu_custom_call" | custom-call | tf_op jit(solution)/shard_map/taylor/pallas_call | solution.py:250
  84.4 1.2 %copy.9 = bf16[1280,640]{1,0:T(8,128)(2,1)} copy(bf16[1280,640]{1,0:T(8,128)(2,1)S(1)} %taylor.1) | data formatting | bytes 3276800
where the time goes:
time: 85.6 us; the launch traced here: 85.5 us
  Pallas kernels  84.4 us (99%)
  local copies, waits for them, and re-layouts  1.17 us (1%)
    pallas_call x1, Pallas kernels, body(): pl.pallas_call(kernel, out_shape=jax.ShapeDtypeStruct(wavefunction.shape,...  84.4 us

commit v1 on v0

--- a/solution.py
+++ b/solution.py
@@ -11,6 +11,7 @@
 PARTS = MAXS // WIDTH
 SPLIT = 384
 UNROLL = 8
+WINDOW = 3
 
 time_step = 0.5
 
@@ -32,6 +33,7 @@
     half,
     early,
     stage,
+    relay,
     x00,
     x01,
     x10,
@@ -46,6 +48,9 @@
     right_sem,
     send_sem,
     recv_sem,
+    hop_send_sem,
+    hop_recv_sem,
+    pass_sem,
 ):
     xs = ((x00, x01), (x10, x11))
     channels = lbuf.shape[1]
@@ -90,48 +95,115 @@
     fetch_left(1).start()
 
     barrier = pltpu.get_barrier_semaphore()
-    for peer in ((me, before), (up, after), (down, before), (me, after)):
-        pl.semaphore_signal(barrier, inc=1, device_id=peer, device_id_type=MESH)
-    pl.semaphore_wait(barrier, 4)
+    has_up, has_down, has_before, has_after = me > 0, me < rows - 1, col > 0, col < cols - 1
+    even = lax.rem(me, 2) == 0
+    peers = (
+        (has_before, (me, before)),
+        (has_after, (me, after)),
+        (has_up & has_after, (up, after)),
+        (has_down & has_before, (down, before)),
+        (has_up & even, (up, col)),
+        (has_down & jnp.logical_not(even), (down, col)),
+    )
+    for present, peer in peers:
+
+        @pl.when(present)
+        def _():
+            pl.semaphore_signal(barrier, inc=1, device_id=peer, device_id_type=MESH)
+
+    pl.semaphore_wait(barrier, sum(present.astype(jnp.int32) for present, _ in peers))
 
     def pieces(t, b, c):
         if t == STEPS - 1 and b == 1 and isinstance(c, int) and c == PARTS - 1:
             return ((c, 0, SPLIT), (PARTS, SPLIT, MAXS - SPLIT))
         return ((c, 0, MAXS),)
 
-    def copies(t, b, c, piece):
+    def relayed(b, c, sender):
+        found = jnp.bool_(False)
+        for z in range(1, rows // 2):
+            count = round((rows // 2 - z) * PARTS / (rows // 2))
+            found = found | ((sender == (2 * z if b == 0 else rows - 1 - 2 * z)) & (c >= PARTS - count))
+        return found & (has_after if b == 0 else has_before)
+
+    def hop(t, b, c):
+        return pltpu.make_async_remote_copy(
+            src_ref=xs[t][b].at[c, 1],
+            dst_ref=relay.at[t, b, c],
+            send_sem=hop_send_sem.at[t, b, c],
+            recv_sem=hop_recv_sem.at[t, b, c],
+            device_id=(up if b == 0 else down, col),
+            device_id_type=MESH,
+        )
+
+    def copy_of(t, b, c, piece, side, passing=False):
         index, first, count = piece
-        targets = ((2, (me if b == 0 else down, before)), (0, (up if b == 0 else me, after)))
-        return [
-            pltpu.make_async_remote_copy(
-                src_ref=xs[t][b].at[c, 1, pl.ds(first, count)],
-                dst_ref=xs[t][1 - b].at[c, slot, pl.ds(first, count)],
-                send_sem=send_sem.at[t, b, index, side],
-                recv_sem=recv_sem.at[t, 1 - b, index, side],
-                device_id=target,
-                device_id_type=MESH,
-            )
-            for side, (slot, target) in enumerate(targets)
-        ]
+        along = (me, before if side == 0 else after)
+        diagonal = (down, before) if b == 1 else (up, after)
+        source = relay.at[t, b, c] if passing else xs[t][b].at[c, 1]
+        return pltpu.make_async_remote_copy(
+            src_ref=source.at[pl.ds(first, count)],
+            dst_ref=xs[t][1 - b].at[c, 2 if side == 0 else 0, pl.ds(first, count)],
+            send_sem=pass_sem.at[t, b, index] if passing else send_sem.at[t, b, index, side],
+            recv_sem=recv_sem.at[t, 1 - b, index, side],
+            device_id=along if side == b or passing else diagonal,
+            device_id_type=MESH,
+        )
+
+    straight = (has_before, has_after)
+    across = (has_up & has_after, has_down & has_before)
+
+    def own(t, b, c, act):
+        for piece in pieces(t, b, c):
+
+            @pl.when(straight[b])
+            def _():
+                act(copy_of(t, b, c, piece, b))
+
+            @pl.when(across[b] & jnp.logical_not(relayed(b, c, me)))
+            def _():
+                act(copy_of(t, b, c, piece, 1 - b))
+
+    def passed(t, b, c, act, arrived=None):
+        @pl.when(relayed(b, c, me + 1 if b == 0 else me - 1))
+        def _():
+            if arrived is not None:
+                arrived(hop(t, b, c))
+            for piece in pieces(t, b, c):
+                act(copy_of(t, b, c, piece, 1 - b, passing=True))
+
+    def begin_hop(t, b, c):
+        @pl.when(relayed(b, c, me))
+        def _():
+            hop(t, b, c).start()
+
+    def start(copy):
+        copy.start()
+
+    def sent(copy):
+        copy.wait_send()
+
+    def landed(copy):
+        copy.wait_recv()
 
     def push(t, b, c):
-        for piece in pieces(t, b, c):
-            for copy in copies(t, b, c, piece):
-                copy.start()
+        own(t, b, c, start)
+        passed(t, b, c, start, landed)
 
     def arrive(t, b, c, piece):
-        for copy in copies(t, 1 - b, c, piece):
-            copy.wait_recv()
+        @pl.when(has_after if b == 1 else has_before)
+        def _():
+            copy_of(t, 1 - b, c, piece, 1 - b).wait_recv()
+
+        @pl.when(has_up & has_after if b == 0 else has_down & has_before)
+        def _():
+            copy_of(t, 1 - b, c, piece, b).wait_recv()
 
     def put(t, b, c, piece):
         span = pl.ds(piece[1], piece[2])
         for slot in range(3):
             stage[slot, span, :] = xs[t][b][c, slot, span, :]
-        no_after, no_before = col == cols - 1, col == 0
-        if b == 0:
-            no_after = no_after | (me == 0)
-        else:
-            no_before = no_before | (me == rows - 1)
+        no_after = jnp.logical_not(has_up & has_after if b == 0 else has_after)
+        no_before = jnp.logical_not(has_before if b == 0 else has_down & has_before)
         for slot, missing in ((2, no_after), (0, no_before)):
 
             @pl.when(missing)
@@ -178,20 +250,54 @@
             fetch_wave(b, c).wait()
             value = xs[0][b][c, 1].astype(jnp.float32)
             xs[0][b][c, 1] = jnp.where(keep(b, c), value, 0.0).astype(jnp.bfloat16)
+            begin_hop(0, b, c)
             if b == 1:
-                push(0, 1, c)
+
+                @pl.when(c < WINDOW)
+                def _():
+                    own(0, 1, c, start)
+
             return carry
 
         lax.fori_loop(0, PARTS, begin, 0)
 
-    for t, b, follow in ((0, 0, (0, 0)), (0, 1, (1, 0)), (1, 1, (1, 1)), (1, 0, None)):
+    def begin_passing(c, carry):
+        passed(0, 1, c, start, landed)
+        return carry
+
+    lax.fori_loop(0, WINDOW, begin_passing, 0)
+
+    order = ((0, 1), (0, 0), (1, 0), (1, 1))
+
+    def advance(phase, c):
+        later = c + WINDOW
+        if isinstance(c, int):
+            if phase + 1 < len(order):
+                push(*order[phase + 1], later - PARTS)
+            return
+
+        if phase + 1 < len(order):
+
+            @pl.when(later >= PARTS)
+            def _():
+                push(*order[phase + 1], later - PARTS)
+
+        @pl.when(later < PARTS - 1)
+        def _():
+            push(*order[phase], later)
+
+        @pl.when(later == PARTS - 1)
+        def _():
+            push(*order[phase], PARTS - 1)
+
+    for phase, (t, b) in enumerate(((0, 0), (0, 1), (1, 1), (1, 0))):
         if t == 0:
             fetch_left(b).wait()
 
         def take(c, piece):
             arrive(t, b, c, piece)
-            if follow is not None and piece[0] is c:
-                push(*follow, c)
+            if piece[0] is c:
+                advance(phase, c)
             if t == 0 and b == 0:
                 fetch_right(c).wait()
             put(t, b, c, piece)
@@ -235,13 +341,29 @@
 
             each_channel(late_channel)
         finish(t, b, acc[...] + second_product(last))
+        if t == 0:
+
+            def next_hop(c, carry):
+                begin_hop(1, b, c)
+                return carry
+
+            lax.fori_loop(0, PARTS, next_hop, 0)
 
     for t in range(STEPS):
         for b in range(2):
-            for c in range(PARTS):
-                for piece in pieces(t, b, c):
-                    for copy in copies(t, b, c, piece):
-                        copy.wait_send()
+
+            def end(c, carry):
+                own(t, b, c, sent)
+                passed(t, b, c, sent)
+
+                @pl.when(relayed(b, c, me))
+                def _():
+                    hop(t, b, c).wait_send()
+
+                return carry
+
+            lax.fori_loop(0, PARTS - 1, end, 0)
+            end(PARTS - 1, 0)
 
 
 def body(wavefunction, left_env, right_env, left_sizes, right_sizes, allowed, channel_shift):
@@ -259,6 +381,7 @@
             pltpu.VMEM((MAXS, channels * WIDTH), jnp.bfloat16),
             pltpu.VMEM((MAXS, channels * WIDTH), jnp.float32),
             pltpu.VMEM((3, MAXS, WIDTH), jnp.bfloat16),
+            pltpu.VMEM((STEPS, 2, PARTS, MAXS, WIDTH), jnp.bfloat16),
             *[pltpu.VMEM((PARTS, 3, MAXS, WIDTH), jnp.bfloat16)] * 4,
             *[pltpu.SMEM(v.shape, v.dtype) for v in arguments[:4]],
             pltpu.SemaphoreType.DMA((4,)),
@@ -267,6 +390,9 @@
             pltpu.SemaphoreType.DMA((PARTS,)),
             pltpu.SemaphoreType.DMA((STEPS, 2, PARTS + 1, 2)),
             pltpu.SemaphoreType.DMA((STEPS, 2, PARTS + 1, 2)),
+            pltpu.SemaphoreType.DMA((STEPS, 2, PARTS)),
+            pltpu.SemaphoreType.DMA((STEPS, 2, PARTS)),
+            pltpu.SemaphoreType.DMA((STEPS, 2, PARTS + 1)),
         ],
         compiler_params=pltpu.CompilerParams(
             collective_id=0, has_side_effects=True, vmem_limit_bytes=52 * 2**20

time: 85.6 us -> 81.4 us (0.951)
  the two profiles are of different devices: /device:TPU:0 before, /device:TPU:55 now
where the time goes in v1:
time: 81.4 us; the launch traced here: 81.3 us
  Pallas kernels  80.2 us (99%)
  local copies, waits for them, and re-layouts  1.17 us (1%)
    pallas_call x1, Pallas kernels, body(): pl.pallas_call(kernel, out_shape=jax.ShapeDtypeStruct(wavefunction.shape,...  80.2 us

profile of v1, /device:TPU:55, one launch (start us, length us, event | category | flops | bytes accessed | tf_op | source)
XLA Modules:
  0.0 81.3 jit_solution(10661934752274229213)
XLA Ops:
  0.0 80.2 %taylor.1 = bf16[1280,640]{1,0:T(8,128)(2,1)S(1)} custom-call(s32[16]{0:T(128)} %left_sizes_in.1, s32[16]{0:T(128)} %right_sizes_in.1, s32[31]{0:T(128)} %allowed_in.1, s32[8]{0:T(128)} %channel_shift_in.1, bf16[1280,640]{1,0:T(8,128)(2,1)} %wave.1, bf16[8,1280,640]{2,1,0:T(8,128)(2,1)} %left_env.1, bf16[8,640,640]{2,1,0:T(8,128)(2,1)} %right_env.1), custom_call_target="tpu_custom_call" | custom-call | tf_op jit(solution)/shard_map/taylor/pallas_call | solution.py:372
  80.2 1.2 %copy.9 = bf16[1280,640]{1,0:T(8,128)(2,1)} copy(bf16[1280,640]{1,0:T(8,128)(2,1)S(1)} %taylor.1) | data formatting | bytes 3276800

commit v2 on v1

--- a/solution.py
+++ b/solution.py
@@ -186,8 +186,8 @@
         copy.wait_recv()
 
     def push(t, b, c):
+        passed(t, b, c, start, landed)
         own(t, b, c, start)
-        passed(t, b, c, start, landed)
 
     def arrive(t, b, c, piece):
         @pl.when(has_after if b == 1 else has_before)

time: 81.4 us -> 81.4 us (level)
  no operation moved by 1% of the time
where the time goes in v2:
time: 81.4 us; the launch traced here: 81.3 us
  Pallas kernels  80.2 us (99%)
  local copies, waits for them, and re-layouts  1.17 us (1%)
    pallas_call x1, Pallas kernels, body(): pl.pallas_call(kernel, out_shape=jax.ShapeDtypeStruct(wavefunction.shape,...  80.2 us

profile of v2, /device:TPU:55, one launch (start us, length us, event | category | flops | bytes accessed | tf_op | source)
XLA Modules:
  0.0 81.3 jit_solution(3336452981230205378)
XLA Ops:
  0.0 80.2 %taylor.1 = bf16[1280,640]{1,0:T(8,128)(2,1)S(1)} custom-call(s32[16]{0:T(128)} %left_sizes_in.1, s32[16]{0:T(128)} %right_sizes_in.1, s32[31]{0:T(128)} %allowed_in.1, s32[8]{0:T(128)} %channel_shift_in.1, bf16[1280,640]{1,0:T(8,128)(2,1)} %wave.1, bf16[8,1280,640]{2,1,0:T(8,128)(2,1)} %left_env.1, bf16[8,640,640]{2,1,0:T(8,128)(2,1)} %right_env.1), custom_call_target="tpu_custom_call" | custom-call | tf_op jit(solution)/shard_map/taylor/pallas_call | solution.py:372
  80.2 1.2 %copy.9 = bf16[1280,640]{1,0:T(8,128)(2,1)} copy(bf16[1280,640]{1,0:T(8,128)(2,1)S(1)} %taylor.1) | data formatting | bytes 3276800
